TPU v7x, 32 devices: a whole 2x2x4 slice. The times are simulated.
32 devices in a mesh: visit: 8 (over y, x, core), row: 4 (over z).
Axes of the slice: x: 2, y: 2, z: 4, core: 2. Of those that a mesh axis runs over, the one named last changes fastest.
Arguments:
- science: float32 [8, 128, 4096], P('visit', 'row'), may hold values from -8 to 8
- basis_kernels: float32 [9, 21, 21], replicated, may hold values from -0.25 to 0.25
- basis_coeffs: float32 [8, 9], P('visit'), may hold values from -2 to 2
- row_starts: int32 [8, 128], P('visit', 'row'), may hold values from -7 to 1
- row_taps: float32 [8, 8, 128], P('visit', None, 'row'), may hold values from -0.2 to 0.45
- col_offsets: int32 [8], P('visit'), may hold values from 0 to 511
- col_starts: int32 [8, 4096], P('visit'), may hold values from -3 to -2
- col_taps: float32 [8, 8, 4096], P('visit'), may hold values from -0.2 to 0.45
- visit_weights: float32 [8], P('visit'), may hold values from 0.25 to 4
- clip_masks: int32 [8, 128, 4096], P('visit', 'row'), may hold values 0 or 1
- decorrelation: float32 [8, 21, 21], P('visit'), may hold values from -0.25 to 0.25
Outputs:
- decorrelated: float32 [8, 128, 4096], P('visit', 'row')
- template: float32 [128, 4096], P('row', 'visit')
Inputs may be any that keep to these rules, and one draw needn't show every extreme that they name: Row i of a visit reads matched rows i + row_starts[v, i] to i + row_starts[v, i] + 7.
All inputs are finite; a program needn't handle non-finite values. No bound on the sum of `clip_masks` on one device may be relied on, other than what follows from the above.
Results may differ from a plain program's by a relative error of at most 0.0003.
Values sent between devices are 32-bit elements; how exact they have to be, the bound alone decides.
A program may use at most 64 MiB of HBM per device.

v0:
```python
import functools

import jax
import jax.numpy as jnp
from jax import lax
from jax.experimental import pallas as pl
from jax.experimental.pallas import tpu as pltpu
from jax.sharding import PartitionSpec as P

KS = 21
HALF = KS // 2
TAPS = 8
PAD = 128
CHUNK = 512
F32 = jnp.float32
BF16 = jnp.bfloat16
MESH = pl.DeviceIdType.MESH
VMEM = pl.BlockSpec(memory_space=pltpu.VMEM)
SMEM = pl.BlockSpec(memory_space=pltpu.SMEM)


def padded_width(columns):
    return -(-(columns + 2 * PAD) // CHUNK) * CHUNK


def split(x):
    high = x.astype(BF16)
    low = (x - high.astype(F32)).astype(BF16)
    return high, low


def toeplitz(kernel_t, c, rows, lead):
    line = jnp.broadcast_to(kernel_t[c : c + 1, :], (rows, 128))
    return pltpu.roll(line, lead, 1, stride=1, stride_axis=0)


def kernel_transposed(kernel, square):
    square[...] = jnp.zeros_like(square)
    square[0:KS, 0:KS] = kernel
    return jnp.transpose(square[...])


def correlate_into(data, hi, lo, partial, emit, rows, depth, group, columns):
    groups = -(-KS // group)
    padded = padded_width(columns)

    @pl.loop(0, padded // CHUNK)
    def _(step):
        start = pl.multiple_of(step * CHUNK, CHUNK)
        window = data[:, pl.ds(start, CHUNK + 128)]
        parts = [window[:, b : b + CHUNK] for b in range(group)]
        parts = [split(part) for part in parts]
        high = jnp.concatenate([part[0] for part in parts], axis=0)
        low = jnp.concatenate([part[1] for part in parts], axis=0)
        total = jnp.dot(hi[...], high, preferred_element_type=F32)
        total = total + jnp.dot(lo[...], high, preferred_element_type=F32)
        total = total + jnp.dot(hi[...], low, preferred_element_type=F32)
        partial[:, pl.ds(start, CHUNK)] = total

    @pl.loop(0, columns // CHUNK)
    def _(step):
        start = pl.multiple_of(step * CHUNK, CHUNK)
        total = jnp.zeros((rows, CHUNK), F32)
        for a in range(groups):
            window = partial[a * rows : (a + 1) * rows, pl.ds(start, CHUNK + 2 * PAD)]
            shift = PAD + group * a - HALF
            total = total + window[:, shift : shift + CHUNK]
        emit(start, total)


def unpack_pair(target, row, packed, columns):
    quarter = columns // 4
    for q in range(4):
        target[row : row + 2, PAD + q * quarter : PAD + (q + 1) * quarter] = packed[2 * q : 2 * q + 2, :]


def pack_pair(packed, source, row, columns):
    quarter = columns // 4
    for q in range(4):
        packed[2 * q : 2 * q + 2, :] = source[row : row + 2, q * quarter : (q + 1) * quarter]


def greet(nv, nr):
    v, r = lax.axis_index("visit"), lax.axis_index("row")
    half = nv // 2
    parity, mine = v % 2, v // 2
    barrier = pltpu.get_barrier_semaphore()

    def hello(a, b):
        pl.semaphore_signal(barrier, inc=1, device_id=(a, b), device_id_type=MESH)

    hello(v + 1 - 2 * parity, r)
    for d in range(1, half):
        hello(2 * ((mine + d) % half) + parity, r)

    @pl.when(r > 0)
    def _():
        hello(v, r - 1)

    @pl.when(r < nr - 1)
    def _():
        hello(v, r + 1)

    above, below = (r > 0).astype(jnp.int32), (r < nr - 1).astype(jnp.int32)
    pl.semaphore_wait(barrier, half + above + below)


def remote(src, dst, send, recv, device):
    return pltpu.make_async_remote_copy(
        src_ref=src, dst_ref=dst, send_sem=send, recv_sem=recv, device_id=device, device_id_type=MESH
    )


def pair_start(nv, blocks, landed, sems):
    v, r = lax.axis_index("visit"), lax.axis_index("row")
    half = nv // 2
    parity, mine = v % 2, v // 2
    copies = {}
    for d in list(range(1, half)) + [0]:
        k = (mine + d) % half
        copies[d] = remote(
            blocks.at[2 * k + 1 - parity], landed.at[k], sems.at[0, d], sems.at[1, d], (v + 1 - 2 * parity, r)
        )
        copies[d].start()
    return copies


def scatter_sum(nv, blocks, landed, pair_copies, sums, arrived, sems):
    v, r = lax.axis_index("visit"), lax.axis_index("row")
    half = nv // 2
    parity, mine = v % 2, v // 2
    copies = []
    for d in range(1, half):
        k = (mine + d) % half
        pair_copies[d].wait()
        sums[d - 1] = blocks[2 * k + parity] + landed[k]
        copy = remote(sums.at[d - 1], arrived.at[d - 1], sems.at[0, d], sems.at[1, d], (2 * k + parity, r))
        copy.start()
        copies.append(copy)
    pair_copies[0].wait()
    total = blocks[v] + landed[mine]
    for d in range(1, half):
        copies[d - 1].wait()
        total = total + arrived[d - 1]
    return total


def sum_scratch(nv, rows, width):
    half = nv // 2
    return [
        pltpu.VMEM((half, rows, width), F32),
        pltpu.VMEM((half - 1, rows, width), F32),
        pltpu.VMEM((half - 1, rows, width), F32),
        pltpu.SemaphoreType.DMA((2, half)),
        pltpu.SemaphoreType.DMA((2, half)),
    ]


def first_kernel(
    nv, nr, science, masks, col_starts, offsets, weights,
    top, top_pair, bottom, bottom_pair, denominator,
    pack_top, pack_bottom, blocks, landed, sums, arrived, pair_sems, sum_sems, halo_sems,
):
    v, r = lax.axis_index("visit"), lax.axis_index("row")
    rows, columns = science.shape
    width = columns // nv
    pack_pair(pack_top, science, 16, columns)
    pack_pair(pack_bottom, science, rows - 18, columns)
    greet(nv, nr)
    up = [
        remote(science.at[0:16], bottom, halo_sems.at[0, 0], halo_sems.at[1, 0], (v, r - 1)),
        remote(pack_top, bottom_pair, halo_sems.at[0, 1], halo_sems.at[1, 1], (v, r - 1)),
    ]
    down = [
        remote(science.at[rows - 16 : rows], top, halo_sems.at[0, 2], halo_sems.at[1, 2], (v, r + 1)),
        remote(pack_bottom, top_pair, halo_sems.at[0, 3], halo_sems.at[1, 3], (v, r + 1)),
    ]

    @pl.when(r > 0)
    def _():
        for copy in up:
            copy.start()

    @pl.when(r < nr - 1)
    def _():
        for copy in down:
            copy.start()

    @pl.when(r == 0)
    def _():
        top[...] = jnp.zeros_like(top)
        top_pair[...] = jnp.zeros_like(top_pair)

    @pl.when(r == nr - 1)
    def _():
        bottom[...] = jnp.zeros_like(bottom)
        bottom_pair[...] = jnp.zeros_like(bottom_pair)

    for u in range(nv):
        span = slice(u * width, (u + 1) * width)
        start = col_starts[:, span] + (
            lax.broadcasted_iota(jnp.int32, (1, width), 1) + (u * width - offsets[0])
        )
        covered = jnp.where((start >= 0) & (start <= columns - TAPS), weights[0], 0.0)
        blocks[u] = masks[:, span].astype(F32) * covered
    pair_copies = pair_start(nv, blocks, landed, pair_sems)
    denominator[...] = scatter_sum(nv, blocks, landed, pair_copies, sums, arrived, sum_sems)

    @pl.when(r > 0)
    def _():
        for copy in up:
            copy.wait_send()
        for copy in down:
            copy.wait_recv()

    @pl.when(r < nr - 1)
    def _():
        for copy in down:
            copy.wait_send()
        for copy in up:
            copy.wait_recv()


def match_kernel(
    science, top, top_pair, bottom, bottom_pair, basis, coeffs, row_starts, row_taps, edges,
    offsets, col_starts, col_taps, weights, masks,
    warped, numerator,
    data, square, flat, hi, lo, partial, shifted,
):
    rows, columns = science.shape
    nv, _, width = numerator.shape
    depth, group = 80, 3
    middle = rows + 2 * TAPS
    data[...] = jnp.zeros_like(data)
    data[8:24, PAD : PAD + columns] = top[...]
    data[24 : 24 + rows, PAD : PAD + columns] = science[...]
    data[24 + rows : 40 + rows, PAD : PAD + columns] = bottom[...]
    unpack_pair(data, 6, top_pair, columns)
    unpack_pair(data, 40 + rows, bottom_pair, columns)
    kernel = coeffs[0] * basis[0]
    for b in range(1, basis.shape[0]):
        kernel = kernel + coeffs[b] * basis[b]
    kernel_t = kernel_transposed(kernel, square)
    m = lax.broadcasted_iota(jnp.int32, (middle, rows), 0) - TAPS
    i = lax.broadcasted_iota(jnp.int32, (middle, rows), 1)
    tap = m - i - row_starts[...]
    inside = (m + edges[0] >= 0) & (m + edges[0] < edges[1])
    mix = jnp.zeros((middle, rows), F32)
    for t in range(TAPS):
        mix = mix + jnp.where((tap == t) & inside, row_taps[t : t + 1, :], 0.0)
    flat[...] = jnp.zeros_like(flat)
    for c in range(KS):
        band = toeplitz(kernel_t, c, middle, 6)
        folded = lax.dot_general(
            mix, band, (((0,), (0,)), ((), ())), precision=lax.Precision.HIGHEST, preferred_element_type=F32
        )
        a, b = c // group, c % group
        flat[a * rows : (a + 1) * rows, b * depth : (b + 1) * depth] = folded[:, :depth]
    high, low = split(flat[...])
    hi[...] = high
    lo[...] = low
    dither = offsets[0]
    tiles = dither // 128
    within = dither % 128
    shifted[...] = jnp.zeros_like(shifted)

    def keep(start, values):
        shifted[:, pl.ds(pl.multiple_of(start + 640, 128), CHUNK)] = values

    correlate_into(data, hi, lo, partial, keep, rows, depth, group, columns)

    @pl.loop(0, nv)
    def _(u):
        start = pl.multiple_of(u * width, width)
        base = pl.multiple_of(start + 384 - tiles * 128, 128)
        window = shifted[:, pl.ds(base, width + 384)]
        window = pltpu.roll(window, within, 1)
        early = col_starts[:, pl.ds(start, width)] == -3
        taps = [col_taps[t : t + 1, pl.ds(start, width)] for t in range(TAPS)]
        total = jnp.zeros((rows, width), F32)
        for lag in range(TAPS + 1):
            now = taps[lag] if lag < TAPS else jnp.zeros_like(taps[0])
            before = taps[lag - 1] if lag > 0 else jnp.zeros_like(taps[0])
            at = 256 + lag - 3
            total = total + jnp.where(early, now, before) * window[:, at : at + width]
        warped[:, pl.ds(start, width)] = total
        first = col_starts[:, pl.ds(start, width)] + (
            lax.broadcasted_iota(jnp.int32, (1, width), 1) + (start - dither)
        )
        covered = jnp.where((first >= 0) & (first <= columns - TAPS), weights[0], 0.0)
        numerator[u] = masks[:, pl.ds(start, width)].astype(F32) * covered * total


def coadd_kernel(
    nv, nr, numerator, denominator, warped,
    template, difference, top, top_pair, bottom, bottom_pair,
    pack_top, pack_bottom, gathered, landed, sums, arrived, pair_sems, sum_sems, gather_sems, pass_sems, halo_sems,
):
    v, r = lax.axis_index("visit"), lax.axis_index("row")
    half = nv // 2
    parity, mine = v % 2, v // 2
    partner = (v + 1 - 2 * parity, r)
    rows, columns = warped.shape
    width = columns // nv
    greet(nv, nr)
    pair_copies = pair_start(nv, numerator, landed, pair_sems)

    @pl.when(r == 0)
    def _():
        top[...] = jnp.zeros_like(top)
        top_pair[...] = jnp.zeros_like(top_pair)

    @pl.when(r == nr - 1)
    def _():
        bottom[...] = jnp.zeros_like(bottom)
        bottom_pair[...] = jnp.zeros_like(bottom_pair)

    total = scatter_sum(nv, numerator, landed, pair_copies, sums, arrived, sum_sems)
    own = total / jnp.maximum(denominator[...], 1.0)
    template[...] = own
    gathered[v] = own
    sends = []
    for d in range(1, half):
        k = (mine + d) % half
        copy = remote(gathered.at[v], gathered.at[v], gather_sems.at[0, d], gather_sems.at[1, d], (2 * k + parity, r))
        copy.start()
        sends.append(copy)

    def passed(d):
        k = (mine + half - d) % half
        u = 2 * k + parity
        return remote(gathered.at[u], gathered.at[u], pass_sems.at[0, d], pass_sems.at[1, d], partner)

    passes = [passed(d) for d in range(half)]
    passes[0].start()

    def halo(u, index, up):
        span = pl.ds(pl.multiple_of(u * width, width), width)
        if up:
            return remote(
                difference.at[0:8, span], bottom.at[:, span],
                halo_sems.at[0, index], halo_sems.at[1, index], (v, r - 1),
            )
        return remote(
            difference.at[rows - 8 : rows, span], top.at[:, span],
            halo_sems.at[2, index], halo_sems.at[3, index], (v, r + 1),
        )

    ups, downs = [], []

    def subtract(u):
        span = pl.ds(pl.multiple_of(u * width, width), width)
        difference[:, span] = warped[:, span] - gathered[u]
        ups.append(halo(u, len(ups), True))
        downs.append(halo(u, len(downs), False))

        @pl.when(r > 0)
        def _():
            ups[-1].start()

        @pl.when(r < nr - 1)
        def _():
            downs[-1].start()

    subtract(v)
    for d in range(half):
        if d > 0:
            sends[d - 1].wait_recv()
            passes[d].start()
            subtract(2 * ((mine + half - d) % half) + parity)
        passes[d].wait_recv()
        subtract(2 * ((mine + half - d) % half) + 1 - parity)
    pack_pair(pack_top, difference, 8, columns)
    pack_pair(pack_bottom, difference, rows - 10, columns)
    ups.append(remote(pack_top, bottom_pair, halo_sems.at[0, nv], halo_sems.at[1, nv], (v, r - 1)))
    downs.append(remote(pack_bottom, top_pair, halo_sems.at[2, nv], halo_sems.at[3, nv], (v, r + 1)))

    @pl.when(r > 0)
    def _():
        ups[-1].start()

    @pl.when(r < nr - 1)
    def _():
        downs[-1].start()

    for copy in sends + passes:
        copy.wait_send()

    @pl.when(r > 0)
    def _():
        for copy in ups:
            copy.wait_send()
        for copy in downs:
            copy.wait_recv()

    @pl.when(r < nr - 1)
    def _():
        for copy in downs:
            copy.wait_send()
        for copy in ups:
            copy.wait_recv()


def clean_kernel(
    difference, top, top_pair, bottom, bottom_pair, decorrelation, cleaned, data, square, flat, hi, lo, partial
):
    rows, columns = difference.shape
    depth, group = 64, 4
    data[...] = jnp.zeros_like(data)
    data[8:16, PAD : PAD + columns] = top[...]
    data[16 : 16 + rows, PAD : PAD + columns] = difference[...]
    data[16 + rows : 24 + rows, PAD : PAD + columns] = bottom[...]
    unpack_pair(data, 6, top_pair, columns)
    unpack_pair(data, 24 + rows, bottom_pair, columns)
    kernel_t = kernel_transposed(decorrelation[...], square)
    flat[...] = jnp.zeros_like(flat)
    for c in range(KS):
        band = toeplitz(kernel_t, c, rows, 6)
        a, b = c // group, c % group
        flat[a * rows : (a + 1) * rows, b * depth : (b + 1) * depth] = band[:, :depth]
    high, low = split(flat[...])
    hi[...] = high
    lo[...] = low

    def keep(start, values):
        cleaned[:, pl.ds(start, CHUNK)] = values

    correlate_into(data, hi, lo, partial, keep, rows, depth, group, columns)


def correlate_scratch(rows, depth, group, columns):
    groups = -(-KS // group)
    padded = padded_width(columns)
    return [
        pltpu.VMEM((depth, padded + 128), F32),
        pltpu.VMEM((128, 128), F32),
        pltpu.VMEM((groups * rows, group * depth), F32),
        pltpu.VMEM((groups * rows, group * depth), BF16),
        pltpu.VMEM((groups * rows, group * depth), BF16),
        pltpu.VMEM((groups * rows, padded), F32),
    ]


def shape(*dims):
    return jax.ShapeDtypeStruct(dims, F32)


def on_device(
    nv, nr, science, basis_kernels, basis_coeffs, row_starts, row_taps, col_offsets,
    col_starts, col_taps, visit_weights, clip_masks, decorrelation,
):
    pixels = science[0]
    masks = clip_masks[0]
    rows, columns = pixels.shape
    width = columns // nv
    limit = 60 * 1024 * 1024
    remote_params = lambda cid: pltpu.CompilerParams(
        collective_id=cid, has_side_effects=True, vmem_limit_bytes=limit
    )
    top, top_pair, bottom, bottom_pair, denominator = pl.pallas_call(
        functools.partial(first_kernel, nv, nr),
        out_shape=(
            shape(16, columns), shape(8, columns // 4), shape(16, columns), shape(8, columns // 4), shape(rows, width)
        ),
        in_specs=[VMEM, VMEM, VMEM, SMEM, SMEM],
        out_specs=(VMEM,) * 5,
        scratch_shapes=[
            pltpu.VMEM((8, columns // 4), F32),
            pltpu.VMEM((8, columns // 4), F32),
            pltpu.VMEM((nv, rows, width), F32),
        ] + sum_scratch(nv, rows, width) + [pltpu.SemaphoreType.DMA((2, 4))],
        compiler_params=remote_params(0),
        name="halo",
    )(pixels, masks, col_starts, col_offsets, visit_weights)
    first_row = lax.axis_index("row") * rows
    edges = jnp.stack([first_row, jnp.int32(rows * nr)])
    warped, numerator = pl.pallas_call(
        match_kernel,
        out_shape=(shape(rows, columns), shape(nv, rows, width)),
        in_specs=[VMEM] * 6 + [SMEM, VMEM, VMEM, SMEM, SMEM, VMEM, VMEM, SMEM, VMEM],
        out_specs=(VMEM, VMEM),
        scratch_shapes=correlate_scratch(rows, 80, 3, columns) + [pltpu.VMEM((rows, columns + 1024), F32)],
        compiler_params=pltpu.CompilerParams(vmem_limit_bytes=limit),
        name="match",
    )(
        pixels, top, top_pair, bottom, bottom_pair, basis_kernels, basis_coeffs[0], row_starts, row_taps[0], edges,
        col_offsets, col_starts, col_taps[0], visit_weights, masks,
    )
    template, difference, top, top_pair, bottom, bottom_pair = pl.pallas_call(
        functools.partial(coadd_kernel, nv, nr),
        out_shape=(
            shape(rows, width), shape(rows, columns),
            shape(8, columns), shape(8, columns // 4), shape(8, columns), shape(8, columns // 4),
        ),
        in_specs=[VMEM] * 3,
        out_specs=(VMEM,) * 6,
        scratch_shapes=[
            pltpu.VMEM((8, columns // 4), F32),
            pltpu.VMEM((8, columns // 4), F32),
            pltpu.VMEM((nv, rows, width), F32),
        ] + sum_scratch(nv, rows, width) + [
            pltpu.SemaphoreType.DMA((2, nv // 2)),
            pltpu.SemaphoreType.DMA((2, nv // 2)),
            pltpu.SemaphoreType.DMA((4, nv + 1)),
        ],
        compiler_params=remote_params(1),
        name="coadd",
    )(numerator, denominator, warped)
    cleaned = pl.pallas_call(
        clean_kernel,
        out_shape=shape(rows, columns),
        in_specs=[VMEM] * 6,
        out_specs=VMEM,
        scratch_shapes=correlate_scratch(rows, 64, 4, columns),
        compiler_params=pltpu.CompilerParams(vmem_limit_bytes=limit),
        name="clean",
    )(difference, top, top_pair, bottom, bottom_pair, decorrelation[0])
    return (cleaned[None], template)


def solution(mesh):
    nv, nr = mesh.shape["visit"], mesh.shape["row"]
    return jax.shard_map(
        functools.partial(on_device, nv, nr),
        mesh=mesh,
        in_specs=(
            P("visit", "row", None),
            P(),
            P("visit", None),
            P("visit", "row"),
            P("visit", None, "row"),
            P("visit"),
            P("visit", None),
            P("visit", None, None),
            P("visit"),
            P("visit", "row", None),
            P("visit", None, None),
        ),
        out_specs=(P("visit", "row", None), P("row", "visit")),
        check_vma=False,
    )
```

profile of v0, /device:TPU:0, one launch (start us, length us, event | category | flops | bytes accessed | tf_op | source)
XLA Modules:
  0.0 60.0 jit_solution(12898627617668514781)
XLA Ops:
  1.9 14.5 %halo.1 = (f32[16,4096]{1,0:T(8,128)}, f32[8,1024]{1,0:T(8,128)}, f32[16,4096]{1,0:T(8,128)}, f32[8,1024]{1,0:T(8,128)}, f32[32,512]{1,0:T(8,128)}) custom-call(f32[32,4096]{1,0:T(8,128)} %bitcast.10, s32[32,4096]{1,0:T(8,128)} %bitcast.12, s32[1,4096]{1,0:T(1,128)} %col_starts.3, s32[1]{0:T(128)S(6)} %copy.17.offsets, f32[1]{0:T(128)S(6)} %copy.18.weights), custom_call_target="tpu_custom_call" | custom-call | tf_op jit(solution)/shard_map/halo/pallas_call | solution.py:460
  16.5 0.6 %pad_add_fusion.edges = s32[2]{0:T(128)} fusion(s32[1]{0:T(128)} %constant.2.clone.1, s32[1]{0:T(128)} %bitcast.4), kind=kLoop, calls=%fused_computation.1 | loop fusion | flops 2 | bytes 16 | tf_op jit(solution)/shard_map/stack | solution.py:476
  17.1 12.2 %match.1 = (f32[32,4096]{1,0:T(8,128)}, f32[8,32,512]{2,1,0:T(8,128)}) custom-call(f32[32,4096]{1,0:T(8,128)} %bitcast.11, f32[16,4096]{1,0:T(8,128)} %get-tuple-element.15.top, f32[8,1024]{1,0:T(8,128)} %get-tuple-element.16.top_pair, f32[16,4096]{1,0:T(8,128)} %get-tuple-element.17.bottom, f32[8,1024]{1,0:T(8,128)} %get-tuple-element.18.bottom_pair, ...), custom_call_target="tpu_custom_call" | custom-call | tf_op jit(solution)/shard_map/match/pallas_call | solution.py:477
  29.3 0.0 copy-start.1
  29.3 21.3 %coadd.1 = (f32[32,512]{1,0:T(8,128)}, f32[32,4096]{1,0:T(8,128)}, f32[8,4096]{1,0:T(8,128)}, f32[8,1024]{1,0:T(8,128)}, f32[8,4096]{1,0:T(8,128)}, /*index=5*/f32[8,1024]{1,0:T(8,128)}) custom-call(f32[8,32,512]{2,1,0:T(8,128)} %get-tuple-element.19.numerator, f32[32,512]{1,0:T(8,128)} %get-tuple-element.20.denominator, f32[32,4096]{1,0:T(8,128)} %get-tuple-element.21.warped), custom_call_target="tpu_custom_call" | custom-call | tf_op jit(solution)/shard_map/coadd/pallas_call | solution.py:489
  50.6 0.0 copy-done.1
  50.6 0.6 %copy.15 = f32[1,21,21]{2,1,0:T(8,128)} copy(f32[1,21,21]{2,0,1:T(1,128)S(1)} %copy-done.1) | data formatting | bytes 3528
  51.2 0.0 copy-start
  51.2 8.2 %clean.1 = f32[32,4096]{1,0:T(8,128)} custom-call(f32[32,4096]{1,0:T(8,128)} %get-tuple-element.22.difference, f32[8,4096]{1,0:T(8,128)} %get-tuple-element.23.top, f32[8,1024]{1,0:T(8,128)} %get-tuple-element.24.top_pair, f32[8,4096]{1,0:T(8,128)} %get-tuple-element.25.bottom, f32[8,1024]{1,0:T(8,128)} %get-tuple-element.26.bottom_pair, f32[21,21]{1,0:T(8,128)} %bitcast.16), custom_call_target="tpu_custom_call" | custom-call | tf_op jit(solution)/shard_map/clean/pallas_call | solution.py:509
  59.4 0.0 copy-done
  59.4 0.6 %copy.19 = f32[32,512]{1,0:T(8,128)} copy(f32[32,512]{1,0:T(8,128)S(1)} %copy-done) | data formatting | bytes 131072
Async XLA Ops:
  29.3 21.3 %copy-start.1 = (f32[1,21,21]{2,0,1:T(1,128)S(1)}, f32[1,21,21]{2,0,1:T(1,128)}, u32[]{:S(2)}) copy-start(f32[1,21,21]{2,0,1:T(1,128)} %param.21) | copy-start | bytes 5296
  51.2 8.2 %copy-start = (f32[32,512]{1,0:T(8,128)S(1)}, f32[32,512]{1,0:T(8,128)}, u32[]{:S(2)}) copy-start(f32[32,512]{1,0:T(8,128)} %get-tuple-element.31) | copy-start | bytes 196612
where the time goes:
time: 60.3 us; the launch traced here: 60 us
  Pallas kernels  56.2 us (93%)
  between operations  1.95 us (3%)
  local copies, waits for them, and re-layouts  1.24 us (2%)
    pallas_call x1, Pallas kernels, on_device(): pl.pallas_call(functools.partial(coadd_kernel, nv, nr), out_shape=(shape(...  21.3 us
    pallas_call x1, Pallas kernels, on_device(): pl.pallas_call(functools.partial(first_kernel, nv, nr), out_shape=(shape(...  14.5 us
    pallas_call x1, Pallas kernels, on_device(): pl.pallas_call(match_kernel, out_shape=(shape(rows, columns), shape(nv, r...  12.2 us
    pallas_call x1, Pallas kernels, on_device(): pl.pallas_call(clean_kernel, out_shape=shape(rows, columns), in_specs=[VM...  8.18 us
    unnamed x6, local copies, waits for them, and re-layouts  1.24 us

commit v1 on v0

v1 whole, which is shorter than its diff:
```python
import functools

import jax
import jax.numpy as jnp
from jax import lax
from jax.experimental import pallas as pl
from jax.experimental.pallas import tpu as pltpu
from jax.sharding import PartitionSpec as P

KS = 21
HALF = KS // 2
TAPS = 8
PAD = 128
CHUNK = 512
F32 = jnp.float32
BF16 = jnp.bfloat16
MESH = pl.DeviceIdType.MESH
VMEM = pl.BlockSpec(memory_space=pltpu.VMEM)
SMEM = pl.BlockSpec(memory_space=pltpu.SMEM)


def padded_width(columns):
    return -(-(columns + 2 * PAD) // CHUNK) * CHUNK


def split(x):
    high = x.astype(BF16)
    low = (x - high.astype(F32)).astype(BF16)
    return high, low


def toeplitz(kernel_t, c, rows, lead):
    line = jnp.broadcast_to(kernel_t[c : c + 1, :], (rows, 128))
    return pltpu.roll(line, lead, 1, stride=1, stride_axis=0)


def kernel_transposed(kernel, square):
    square[...] = jnp.zeros_like(square)
    square[0:KS, 0:KS] = kernel
    return jnp.transpose(square[...])


def piece(high, low, hi, lo, partial, start, group, add=False):
    m = hi.shape[0]
    window_h = high[:, start : start + CHUNK + 128]
    window_l = low[:, start : start + CHUNK + 128]
    stack_h = jnp.concatenate([window_h[:, b : b + CHUNK] for b in range(group)], axis=0)
    stack_l = jnp.concatenate([window_l[:, b : b + CHUNK] for b in range(group)], axis=0)
    total = jnp.dot(hi[...], stack_h, preferred_element_type=F32)
    total = total + jnp.dot(lo[...], stack_h, preferred_element_type=F32)
    total = total + jnp.dot(hi[...], stack_l, preferred_element_type=F32)
    if add:
        total = total + partial[0:m, start : start + CHUNK]
    partial[0:m, start : start + CHUNK] = total


def shifted_sum(partial, start, rows, group):
    total = jnp.zeros((rows, CHUNK), F32)
    for a in range(-(-KS // group)):
        window = partial[a * rows : (a + 1) * rows, start : start + CHUNK + 2 * PAD]
        shift = PAD + group * a - HALF
        total = total + window[:, shift : shift + CHUNK]
    return total


def store_split(high, low, row, column, values):
    h, l = split(values)
    high[row : row + values.shape[0], column : column + values.shape[1]] = h
    low[row : row + values.shape[0], column : column + values.shape[1]] = l


def pack_pair(packed, source, row, columns):
    quarter = columns // 4
    for q in range(4):
        packed[2 * q : 2 * q + 2, :] = source[row : row + 2, q * quarter : (q + 1) * quarter]


def greet(nv, nr):
    v, r = lax.axis_index("visit"), lax.axis_index("row")
    half = nv // 2
    parity, mine = v % 2, v // 2
    barrier = pltpu.get_barrier_semaphore()

    def hello(a, b):
        pl.semaphore_signal(barrier, inc=1, device_id=(a, b), device_id_type=MESH)

    hello(v + 1 - 2 * parity, r)
    for d in range(1, half):
        hello(2 * ((mine + d) % half) + parity, r)

    @pl.when(r > 0)
    def _():
        hello(v, r - 1)

    @pl.when(r < nr - 1)
    def _():
        hello(v, r + 1)

    above, below = (r > 0).astype(jnp.int32), (r < nr - 1).astype(jnp.int32)
    pl.semaphore_wait(barrier, half + above + below)


def remote(src, dst, send, recv, device):
    return pltpu.make_async_remote_copy(
        src_ref=src, dst_ref=dst, send_sem=send, recv_sem=recv, device_id=device, device_id_type=MESH
    )


def pair_start(nv, blocks, landed, sems):
    v, r = lax.axis_index("visit"), lax.axis_index("row")
    half = nv // 2
    parity, mine = v % 2, v // 2
    copies = {}
    for d in list(range(1, half)) + [0]:
        k = (mine + d) % half
        copies[d] = remote(
            blocks.at[2 * k + 1 - parity], landed.at[k], sems.at[0, d], sems.at[1, d], (v + 1 - 2 * parity, r)
        )
        copies[d].start()
    return copies


def scatter_sum(nv, blocks, landed, pair_copies, sums, arrived, sems):
    v, r = lax.axis_index("visit"), lax.axis_index("row")
    half = nv // 2
    parity, mine = v % 2, v // 2
    copies = []
    for d in range(1, half):
        k = (mine + d) % half
        pair_copies[d].wait()
        sums[d - 1] = blocks[2 * k + parity] + landed[k]
        copy = remote(sums.at[d - 1], arrived.at[d - 1], sems.at[0, d], sems.at[1, d], (2 * k + parity, r))
        copy.start()
        copies.append(copy)
    pair_copies[0].wait()
    total = blocks[v] + landed[mine]
    for d in range(1, half):
        copies[d - 1].wait()
        total = total + arrived[d - 1]
    return total


def exchange_scratch(nv, rows, width):
    half = nv // 2
    return [
        pltpu.VMEM((half, rows, width), F32),
        pltpu.VMEM((half, rows, width), F32),
        pltpu.VMEM((half, rows, width), F32),
        pltpu.SemaphoreType.DMA((2, half)),
        pltpu.SemaphoreType.DMA((2, half)),
    ]


def whole_kernel(
    nv, nr, science, basis, coeffs, row_starts, row_taps, offsets, col_starts, col_taps, weights, masks, decor,
    cleaned, template,
    shares, numerators, warped, difference, gathered, denominator,
    near_top, near_bottom, packs, pairs_top, pairs_bottom,
    late_top, late_bottom, late_pack_top, late_pack_bottom, late_pair_top, late_pair_bottom,
    square, bands, flat, hi, lo, flat_own, own_hi, own_lo, flat_edge, edge_hi, edge_lo,
    high, low, second_high, second_low, edge_high, edge_low, partial, shifted, mover,
    d_landed, d_sums, d_arrived, d_pair, d_sum,
    n_landed, n_sums, n_arrived, n_pair, n_sum,
    gather_sems, pass_sems, halo_sems, late_sems,
):
    v, r = lax.axis_index("visit"), lax.axis_index("row")
    rows, columns = science.shape
    width = columns // nv
    half = nv // 2
    parity, mine = v % 2, v // 2
    partner = (v + 1 - 2 * parity, r)
    chunks = packs.shape[1]
    span = columns // chunks
    padded = padded_width(columns)
    depth, group = high.shape[0], 3
    middle = rows + 2 * TAPS

    quarter = span // 4
    for n in range(chunks):
        for q in range(4):
            at = n * span + q * quarter
            packs[0, n, 2 * q : 2 * q + 2, :] = science[16:18, at : at + quarter]
            packs[1, n, 2 * q : 2 * q + 2, :] = science[rows - 18 : rows - 16, at : at + quarter]
    greet(nv, nr)
    up, down = [], []
    for n in range(chunks):
        cols = slice(n * span, (n + 1) * span)
        up.append(remote(science.at[0:16, cols], near_bottom.at[:, cols], halo_sems.at[0, n], halo_sems.at[1, n], (v, r - 1)))
        up.append(remote(packs.at[0, n], pairs_bottom.at[n], halo_sems.at[2, n], halo_sems.at[3, n], (v, r - 1)))
        down.append(remote(science.at[rows - 16 : rows, cols], near_top.at[:, cols], halo_sems.at[4, n], halo_sems.at[5, n], (v, r + 1)))
        down.append(remote(packs.at[1, n], pairs_top.at[n], halo_sems.at[6, n], halo_sems.at[7, n], (v, r + 1)))

    @pl.when(r > 0)
    def _():
        for copy in up:
            copy.start()

    @pl.when(r < nr - 1)
    def _():
        for copy in down:
            copy.start()

    @pl.when(r == 0)
    def _():
        near_top[...] = jnp.zeros_like(near_top)
        pairs_top[...] = jnp.zeros_like(pairs_top)
        late_top[...] = jnp.zeros_like(late_top)
        late_pair_top[...] = jnp.zeros_like(late_pair_top)

    @pl.when(r == nr - 1)
    def _():
        near_bottom[...] = jnp.zeros_like(near_bottom)
        pairs_bottom[...] = jnp.zeros_like(pairs_bottom)
        late_bottom[...] = jnp.zeros_like(late_bottom)
        late_pair_bottom[...] = jnp.zeros_like(late_pair_bottom)

    dither = offsets[0]
    for u in range(nv):
        cols = slice(u * width, (u + 1) * width)
        start = col_starts[:, cols] + (lax.broadcasted_iota(jnp.int32, (1, width), 1) + (u * width - dither))
        covered = jnp.where((start >= 0) & (start <= columns - TAPS), weights[0], 0.0)
        shares[u] = masks[:, cols].astype(F32) * covered
    weight_pairs = pair_start(nv, shares, d_landed, d_pair)

    kernel = coeffs[0] * basis[0]
    for b in range(1, basis.shape[0]):
        kernel = kernel + coeffs[b] * basis[b]
    kernel_t = kernel_transposed(kernel, square)
    m = lax.broadcasted_iota(jnp.int32, (middle, rows), 0) - TAPS
    i = lax.broadcasted_iota(jnp.int32, (middle, rows), 1)
    tap = m - i - row_starts[...]
    inside = (m + r * rows >= 0) & (m + r * rows < nr * rows)
    mix = jnp.zeros((middle, rows), F32)
    for t in range(TAPS):
        mix = mix + jnp.where((tap == t) & inside, row_taps[t : t + 1, :], 0.0)
    for c in range(KS):
        bands[:, c * 128 : (c + 1) * 128] = toeplitz(kernel_t, c, middle, 6)
    folded = lax.dot_general(
        mix, bands[...], (((0,), (0,)), ((), ())), precision=lax.Precision.HIGHEST, preferred_element_type=F32
    )
    flat[...] = jnp.zeros_like(flat)
    for c in range(KS):
        a, b = c // group, c % group
        flat[a * rows : (a + 1) * rows, b * depth : (b + 1) * depth] = folded[:, c * 128 : c * 128 + depth]
    h, l = split(flat[...])
    hi[...] = h
    lo[...] = l

    kernel_t = kernel_transposed(decor[:, 0, :], square)
    flat_own[...] = jnp.zeros_like(flat_own)
    flat_edge[...] = jnp.zeros_like(flat_edge)
    for c in range(KS):
        band = toeplitz(kernel_t, c, rows, 6)
        a, b = c // 8, c % 8
        here = slice(a * rows, (a + 1) * rows)
        flat_own[here, b * rows : (b + 1) * rows] = band[:, 16 : 16 + rows]
        flat_edge[here, b * 32 : b * 32 + 16] = band[:, 0:16]
        flat_edge[here, b * 32 + 16 : b * 32 + 32] = band[:, 16 + rows : 32 + rows]
    h, l = split(flat_own[...])
    own_hi[...] = h
    own_lo[...] = l
    h, l = split(flat_edge[...])
    edge_hi[...] = h
    edge_lo[...] = l

    for frame in (high, low, second_high, second_low, edge_high, edge_low):
        frame[...] = jnp.zeros_like(frame)
    shifted[...] = jnp.zeros_like(shifted)
    denominator[...] = scatter_sum(nv, shares, d_landed, weight_pairs, d_sums, d_arrived, d_sum)

    tiles = jnp.full((rows, width + 384), dither // 128, jnp.int32)
    place = lax.broadcasted_iota(jnp.int32, (256, 128), 0) - lax.broadcasted_iota(jnp.int32, (256, 128), 1)
    mover[...] = jnp.where(place == 128 - dither % 128, 1.0, 0.0).astype(BF16)

    def warp(u):
        start = u * width
        count = width // 128 + 2
        window = shifted[:, start + 384 : start + 768 + width]
        for t in range(1, 4):
            at = start + 384 - 128 * t
            window = jnp.where(tiles == t, shifted[:, at : at + width + 384], window)
        h, l = split(window)
        stack_h = jnp.concatenate([h[:, 128 * j : 128 * j + 256] for j in range(count)], axis=0)
        stack_l = jnp.concatenate([l[:, 128 * j : 128 * j + 256] for j in range(count)], axis=0)
        moved = jnp.dot(stack_h, mover[...], preferred_element_type=F32)
        moved = moved + jnp.dot(stack_l, mover[...], preferred_element_type=F32)
        window = jnp.concatenate([moved[j * rows : (j + 1) * rows] for j in range(count)], axis=1)
        cols = slice(start, start + width)
        early = col_starts[:, cols] == -3
        taps = [col_taps[t : t + 1, cols] for t in range(TAPS)]
        total = jnp.zeros((rows, width), F32)
        for lag in range(TAPS + 1):
            now = taps[lag] if lag < TAPS else jnp.zeros_like(taps[0])
            before = taps[lag - 1] if lag > 0 else jnp.zeros_like(taps[0])
            at = 128 + lag - 3
            total = total + jnp.where(early, now, before) * window[:, at : at + width]
        warped[:, cols] = total
        numerators[u] = shares[u] * total

    def number_pair(k):
        return remote(numerators.at[2 * k + 1 - parity], n_landed.at[k], n_pair.at[0, k], n_pair.at[1, k], partner)

    def number_sum(k, d):
        return remote(n_sums.at[k], n_arrived.at[d], n_sum.at[0, d], n_sum.at[1, d], (2 * k + parity, r))

    def forward(k):
        number_pair(k).wait()
        n_sums[k] = numerators[2 * k + parity] + n_landed[k]
        d = (k - mine + half) % half

        @pl.when(d > 0)
        def _():
            number_sum(k, d).start()

    pieces = padded // CHUNK
    done_pieces, done_sums, done_warps, done_pairs, done_forwards = 0, 0, 0, 0, 0
    for n in range(chunks):
        cols = slice(n * span, (n + 1) * span)

        @pl.when(r > 0)
        def _():
            down[2 * n].wait_recv()
            down[2 * n + 1].wait_recv()

        @pl.when(r < nr - 1)
        def _():
            up[2 * n].wait_recv()
            up[2 * n + 1].wait_recv()

        store_split(high, low, 24, PAD + n * span, science[:, cols])
        top = near_top[:, cols]
        bottom = near_bottom[:, cols]
        store_split(high, low, 8, PAD + n * span, top)
        store_split(high, low, 24 + rows, PAD + n * span, bottom)
        for q in range(4):
            at = PAD + n * span + q * quarter
            store_split(high, low, 6, at, pairs_top[n, 2 * q : 2 * q + 2, :])
            store_split(high, low, 40 + rows, at, pairs_bottom[n, 2 * q : 2 * q + 2, :])
        last = n == chunks - 1
        while done_pieces < pieces and (last or (done_pieces + 1) * CHUNK + group - PAD <= (n + 1) * span):
            piece(high, low, hi, lo, partial, done_pieces * CHUNK, group)
            done_pieces += 1
        while done_sums < columns // CHUNK and done_sums + 2 <= done_pieces:
            start = done_sums * CHUNK
            shifted[:, 640 + start : 640 + start + CHUNK] = shifted_sum(partial, start, rows, group)
            done_sums += 1
        while done_warps < nv and (done_sums * CHUNK >= (done_warps + 1) * width + 8 or done_sums * CHUNK == columns):
            warp(done_warps)
            done_warps += 1
            if done_warps % 2 == 0:
                number_pair(done_pairs).start()
                done_pairs += 1
                if done_pairs >= 2:
                    forward(done_forwards)
                    done_forwards += 1
    while done_forwards < half:
        forward(done_forwards)
        done_forwards += 1

    total = n_sums[mine]
    for d in range(1, half):
        number_sum((mine + d) % half, d).wait()
        total = total + n_arrived[d]
    own = total / jnp.maximum(denominator[...], 1.0)
    template[...] = own
    gathered[v] = own
    sends = []
    for d in range(1, half):
        k = (mine + d) % half
        copy = remote(gathered.at[v], gathered.at[v], gather_sems.at[0, d], gather_sems.at[1, d], (2 * k + parity, r))
        copy.start()
        sends.append(copy)

    def passed(d):
        u = 2 * ((mine + half - d) % half) + parity
        return remote(gathered.at[u], gathered.at[u], pass_sems.at[0, d], pass_sems.at[1, d], partner)

    passes = [passed(d) for d in range(half)]
    passes[0].start()
    ups, downs = [], []

    def subtract(u):
        cols = pl.ds(pl.multiple_of(u * width, width), width)
        at = pl.ds(pl.multiple_of(PAD + u * width, 128), width)
        values = warped[:, cols] - gathered[u]
        difference[:, cols] = values
        h, l = split(values)
        second_high[:, at] = h
        second_low[:, at] = l
        n = len(ups)
        ups.append(remote(difference.at[0:8, cols], late_bottom.at[:, cols], late_sems.at[0, n], late_sems.at[1, n], (v, r - 1)))
        downs.append(
            remote(difference.at[rows - 8 : rows, cols], late_top.at[:, cols], late_sems.at[2, n], late_sems.at[3, n], (v, r + 1))
        )

        @pl.when(r > 0)
        def _():
            ups[-1].start()

        @pl.when(r < nr - 1)
        def _():
            downs[-1].start()

    subtract(v)
    for d in range(half):
        if d > 0:
            sends[d - 1].wait_recv()
            passes[d].start()
            subtract(2 * ((mine + half - d) % half) + parity)
        passes[d].wait_recv()
        subtract(2 * ((mine + half - d) % half) + 1 - parity)
    pack_pair(late_pack_top, difference, 8, columns)
    pack_pair(late_pack_bottom, difference, rows - 10, columns)
    ups.append(remote(late_pack_top, late_pair_bottom, late_sems.at[0, nv], late_sems.at[1, nv], (v, r - 1)))
    downs.append(remote(late_pack_bottom, late_pair_top, late_sems.at[2, nv], late_sems.at[3, nv], (v, r + 1)))

    @pl.when(r > 0)
    def _():
        ups[-1].start()

    @pl.when(r < nr - 1)
    def _():
        downs[-1].start()

    for n in range(pieces):
        piece(second_high, second_low, own_hi, own_lo, partial, n * CHUNK, 8)

    @pl.when(r > 0)
    def _():
        for copy in downs:
            copy.wait_recv()

    @pl.when(r < nr - 1)
    def _():
        for copy in ups:
            copy.wait_recv()

    store_split(edge_high, edge_low, 8, PAD, late_top[...])
    store_split(edge_high, edge_low, 16, PAD, late_bottom[...])
    for q in range(4):
        at = PAD + q * (columns // 4)
        store_split(edge_high, edge_low, 6, at, late_pair_top[2 * q : 2 * q + 2, :])
        store_split(edge_high, edge_low, 24, at, late_pair_bottom[2 * q : 2 * q + 2, :])
    for n in range(pieces):
        piece(edge_high, edge_low, edge_hi, edge_lo, partial, n * CHUNK, 8, add=True)
        if n > 0 and n * CHUNK <= columns:
            cleaned[:, (n - 1) * CHUNK : n * CHUNK] = shifted_sum(partial, (n - 1) * CHUNK, rows, 8)

    for copy in sends + passes:
        copy.wait_send()

    @pl.when(r > 0)
    def _():
        for copy in up + ups:
            copy.wait_send()

    @pl.when(r < nr - 1)
    def _():
        for copy in down + downs:
            copy.wait_send()


def shape(*dims):
    return jax.ShapeDtypeStruct(dims, F32)


def on_device(
    nv, nr, science, basis_kernels, basis_coeffs, row_starts, row_taps, col_offsets,
    col_starts, col_taps, visit_weights, clip_masks, decorrelation,
):
    pixels = science[0]
    rows, columns = pixels.shape
    width = columns // nv
    half = nv // 2
    chunks = 4
    span = columns // chunks
    padded = padded_width(columns)
    depth, group = 80, 3
    tall = -(-KS // group) * rows
    wide = -(-KS // 8) * rows
    f32 = lambda *dims: pltpu.VMEM(dims, F32)
    bf16 = lambda *dims: pltpu.VMEM(dims, BF16)
    cleaned, template = pl.pallas_call(
        functools.partial(whole_kernel, nv, nr),
        out_shape=(shape(rows, columns), shape(rows, width)),
        in_specs=[VMEM, VMEM, SMEM, VMEM, VMEM, SMEM, VMEM, VMEM, SMEM, VMEM, VMEM],
        out_specs=(VMEM, VMEM),
        scratch_shapes=[
            f32(nv, rows, width), f32(nv, rows, width), f32(rows, columns), f32(rows, columns),
            f32(nv, rows, width), f32(rows, width),
            f32(16, columns), f32(16, columns), f32(2, chunks, 8, span // 4),
            f32(chunks, 8, span // 4), f32(chunks, 8, span // 4),
            f32(8, columns), f32(8, columns), f32(8, columns // 4), f32(8, columns // 4),
            f32(8, columns // 4), f32(8, columns // 4),
            f32(128, 128), f32(rows + 2 * TAPS, KS * 128),
            f32(tall, group * depth), bf16(tall, group * depth), bf16(tall, group * depth),
            f32(wide, 8 * rows), bf16(wide, 8 * rows), bf16(wide, 8 * rows),
            f32(wide, 256), bf16(wide, 256), bf16(wide, 256),
            bf16(depth, padded + 128), bf16(depth, padded + 128),
            bf16(rows, padded + 128), bf16(rows, padded + 128),
            bf16(32, padded + 128), bf16(32, padded + 128),
            f32(tall, padded), f32(rows, columns + 1024), bf16(256, 128),
        ] + exchange_scratch(nv, rows, width) + exchange_scratch(nv, rows, width) + [
            pltpu.SemaphoreType.DMA((2, half)),
            pltpu.SemaphoreType.DMA((2, half)),
            pltpu.SemaphoreType.DMA((8, chunks)),
            pltpu.SemaphoreType.DMA((4, nv + 1)),
        ],
        compiler_params=pltpu.CompilerParams(
            collective_id=0, has_side_effects=True, vmem_limit_bytes=60 * 1024 * 1024
        ),
        name="whole",
    )(
        pixels, basis_kernels, basis_coeffs[0], row_starts, row_taps[0], col_offsets, col_starts, col_taps[0],
        visit_weights, clip_masks[0], jnp.transpose(decorrelation, (1, 0, 2)),
    )
    return (cleaned[None], template)


def solution(mesh):
    nv, nr = mesh.shape["visit"], mesh.shape["row"]
    return jax.shard_map(
        functools.partial(on_device, nv, nr),
        mesh=mesh,
        in_specs=(
            P("visit", "row", None),
            P(),
            P("visit", None),
            P("visit", "row"),
            P("visit", None, "row"),
            P("visit"),
            P("visit", None),
            P("visit", None, None),
            P("visit"),
            P("visit", "row", None),
            P("visit", None, None),
        ),
        out_specs=(P("visit", "row", None), P("row", "visit")),
        check_vma=False,
    )
```

time: 60.3 us -> 44 us (0.73)
  Pallas kernels: 56.2 us -> 39.3 us
  local copies, waits for them, and re-layouts: 1.24 us -> 2.53 us
    pallas_call x4 -> x1, Pallas kernels: 56.2 us -> 39.3 us  [on_device(): pl.pallas_call(functools.partial(whole_kernel, nv, nr), out_shape=(shape(...]
    unnamed x6 -> x4, local copies, waits for them, and re-layouts: 1.24 us -> 2.53 us
where the time goes in v1:
time: 44 us; the launch traced here: 43.8 us
  Pallas kernels  39.3 us (89%)
  local copies, waits for them, and re-layouts  2.53 us (6%)
  between operations  1.94 us (4%)
    pallas_call x1, Pallas kernels, on_device(): pl.pallas_call(functools.partial(whole_kernel, nv, nr), out_shape=(shape(...  39.3 us
    unnamed x4, local copies, waits for them, and re-layouts  2.53 us

profile of v1, /device:TPU:0, one launch (start us, length us, event | category | flops | bytes accessed | tf_op | source)
XLA Modules:
  0.0 43.8 jit_solution(7301454165586004445)
XLA Ops:
  1.9 39.3 %whole.1 = (f32[32,4096]{1,0:T(8,128)}, f32[32,512]{1,0:T(8,128)}) custom-call(f32[32,4096]{1,0:T(8,128)} %bitcast.7, f32[9,21,21]{2,1,0:T(8,128)} %basis.1, f32[9]{0:T(128)} %bitcast.13, s32[1,32]{1,0:T(1,128)} %row_starts.1, f32[8,32]{1,0:T(8,128)} %bitcast.12, s32[1]{0:T(128)S(6)} %copy.15.offsets, s32[1,4096]{1,0:T(1,128)} %col_starts.1, ...), custom_call_target="tpu_custom_call" | custom-call | tf_op jit(solution)/shard_map/whole/pallas_call | solution.py:483
  41.3 0.0 copy-start
  41.3 1.9 %copy.17 = f32[1,32,4096]{2,1,0:T(8,128)} copy(f32[1,32,4096]{2,1,0:T(8,128)} %bitcast.9) | data formatting | bytes 1048576
  43.2 0.0 copy-done
  43.2 0.6 %copy.18 = f32[32,512]{1,0:T(8,128)} copy(f32[32,512]{1,0:T(8,128)S(1)} %copy-done) | data formatting | bytes 131072
Async XLA Ops:
  41.3 1.9 %copy-start = (f32[32,512]{1,0:T(8,128)S(1)}, f32[32,512]{1,0:T(8,128)}, u32[]{:S(2)}) copy-start(f32[32,512]{1,0:T(8,128)} %get-tuple-element.9) | copy-start | bytes 196612

commit v2 on v1

--- a/solution.py
+++ b/solution.py
@@ -40,15 +40,14 @@
     return jnp.transpose(square[...])
 
 
-def piece(high, low, hi, lo, partial, start, group, add=False):
-    m = hi.shape[0]
+def piece(high, low, both, partial, start, group, add=False):
+    m = both.shape[0]
     window_h = high[:, start : start + CHUNK + 128]
     window_l = low[:, start : start + CHUNK + 128]
-    stack_h = jnp.concatenate([window_h[:, b : b + CHUNK] for b in range(group)], axis=0)
-    stack_l = jnp.concatenate([window_l[:, b : b + CHUNK] for b in range(group)], axis=0)
-    total = jnp.dot(hi[...], stack_h, preferred_element_type=F32)
-    total = total + jnp.dot(lo[...], stack_h, preferred_element_type=F32)
-    total = total + jnp.dot(hi[...], stack_l, preferred_element_type=F32)
+    stack_h = [window_h[:, b : b + CHUNK] for b in range(group)]
+    stack_l = [window_l[:, b : b + CHUNK] for b in range(group)]
+    stack = jnp.concatenate(stack_h + stack_l + stack_h, axis=0)
+    total = jnp.dot(both[...], stack, preferred_element_type=F32)
     if add:
         total = total + partial[0:m, start : start + CHUNK]
     partial[0:m, start : start + CHUNK] = total
@@ -69,6 +68,14 @@
     low[row : row + values.shape[0], column : column + values.shape[1]] = l
 
 
+def store_both(both, values):
+    h, l = split(values)
+    k = values.shape[1]
+    both[:, 0:k] = h
+    both[:, k : 2 * k] = h
+    both[:, 2 * k : 3 * k] = l
+
+
 def pack_pair(packed, source, row, columns):
     quarter = columns // 4
     for q in range(4):
@@ -96,8 +103,11 @@
     def _():
         hello(v, r + 1)
 
+
+def greeted(nv, nr):
+    r = lax.axis_index("row")
     above, below = (r > 0).astype(jnp.int32), (r < nr - 1).astype(jnp.int32)
-    pl.semaphore_wait(barrier, half + above + below)
+    pl.semaphore_wait(pltpu.get_barrier_semaphore(), nv // 2 + above + below)
 
 
 def remote(src, dst, send, recv, device):
@@ -157,7 +167,7 @@
     shares, numerators, warped, difference, gathered, denominator,
     near_top, near_bottom, packs, pairs_top, pairs_bottom,
     late_top, late_bottom, late_pack_top, late_pack_bottom, late_pair_top, late_pair_bottom,
-    square, bands, flat, hi, lo, flat_own, own_hi, own_lo, flat_edge, edge_hi, edge_lo,
+    square, bands, flat, both, flat_own, own_both, flat_edge, edge_both,
     high, low, second_high, second_low, edge_high, edge_low, partial, shifted, mover,
     d_landed, d_sums, d_arrived, d_pair, d_sum,
     n_landed, n_sums, n_arrived, n_pair, n_sum,
@@ -175,13 +185,21 @@
     depth, group = high.shape[0], 3
     middle = rows + 2 * TAPS
 
+    greet(nv, nr)
+    dither = offsets[0]
+    for u in range(nv):
+        cols = slice(u * width, (u + 1) * width)
+        start = col_starts[:, cols] + (lax.broadcasted_iota(jnp.int32, (1, width), 1) + (u * width - dither))
+        covered = jnp.where((start >= 0) & (start <= columns - TAPS), weights[0], 0.0)
+        shares[u] = masks[:, cols].astype(F32) * covered
+
     quarter = span // 4
     for n in range(chunks):
         for q in range(4):
             at = n * span + q * quarter
             packs[0, n, 2 * q : 2 * q + 2, :] = science[16:18, at : at + quarter]
             packs[1, n, 2 * q : 2 * q + 2, :] = science[rows - 18 : rows - 16, at : at + quarter]
-    greet(nv, nr)
+    greeted(nv, nr)
     up, down = [], []
     for n in range(chunks):
         cols = slice(n * span, (n + 1) * span)
@@ -214,12 +232,6 @@
         late_bottom[...] = jnp.zeros_like(late_bottom)
         late_pair_bottom[...] = jnp.zeros_like(late_pair_bottom)
 
-    dither = offsets[0]
-    for u in range(nv):
-        cols = slice(u * width, (u + 1) * width)
-        start = col_starts[:, cols] + (lax.broadcasted_iota(jnp.int32, (1, width), 1) + (u * width - dither))
-        covered = jnp.where((start >= 0) & (start <= columns - TAPS), weights[0], 0.0)
-        shares[u] = masks[:, cols].astype(F32) * covered
     weight_pairs = pair_start(nv, shares, d_landed, d_pair)
 
     kernel = coeffs[0] * basis[0]
@@ -242,9 +254,7 @@
     for c in range(KS):
         a, b = c // group, c % group
         flat[a * rows : (a + 1) * rows, b * depth : (b + 1) * depth] = folded[:, c * 128 : c * 128 + depth]
-    h, l = split(flat[...])
-    hi[...] = h
-    lo[...] = l
+    store_both(both, flat[...])
 
     kernel_t = kernel_transposed(decor[:, 0, :], square)
     flat_own[...] = jnp.zeros_like(flat_own)
@@ -256,12 +266,8 @@
         flat_own[here, b * rows : (b + 1) * rows] = band[:, 16 : 16 + rows]
         flat_edge[here, b * 32 : b * 32 + 16] = band[:, 0:16]
         flat_edge[here, b * 32 + 16 : b * 32 + 32] = band[:, 16 + rows : 32 + rows]
-    h, l = split(flat_own[...])
-    own_hi[...] = h
-    own_lo[...] = l
-    h, l = split(flat_edge[...])
-    edge_hi[...] = h
-    edge_lo[...] = l
+    store_both(own_both, flat_own[...])
+    store_both(edge_both, flat_edge[...])
 
     for frame in (high, low, second_high, second_low, edge_high, edge_low):
         frame[...] = jnp.zeros_like(frame)
@@ -338,7 +344,7 @@
             store_split(high, low, 40 + rows, at, pairs_bottom[n, 2 * q : 2 * q + 2, :])
         last = n == chunks - 1
         while done_pieces < pieces and (last or (done_pieces + 1) * CHUNK + group - PAD <= (n + 1) * span):
-            piece(high, low, hi, lo, partial, done_pieces * CHUNK, group)
+            piece(high, low, both, partial, done_pieces * CHUNK, group)
             done_pieces += 1
         while done_sums < columns // CHUNK and done_sums + 2 <= done_pieces:
             start = done_sums * CHUNK
@@ -423,7 +429,7 @@
         downs[-1].start()
 
     for n in range(pieces):
-        piece(second_high, second_low, own_hi, own_lo, partial, n * CHUNK, 8)
+        piece(second_high, second_low, own_both, partial, n * CHUNK, 8)
 
     @pl.when(r > 0)
     def _():
@@ -442,7 +448,7 @@
         store_split(edge_high, edge_low, 6, at, late_pair_top[2 * q : 2 * q + 2, :])
         store_split(edge_high, edge_low, 24, at, late_pair_bottom[2 * q : 2 * q + 2, :])
     for n in range(pieces):
-        piece(edge_high, edge_low, edge_hi, edge_lo, partial, n * CHUNK, 8, add=True)
+        piece(edge_high, edge_low, edge_both, partial, n * CHUNK, 8, add=True)
         if n > 0 and n * CHUNK <= columns:
             cleaned[:, (n - 1) * CHUNK : n * CHUNK] = shifted_sum(partial, (n - 1) * CHUNK, rows, 8)
 
@@ -458,6 +464,11 @@
     def _():
         for copy in down + downs:
             copy.wait_send()
+
+
+def hand_over(cleaned, template, cleaned_out, template_out):
+    cleaned_out[...] = cleaned[...]
+    template_out[...] = template[...]
 
 
 def shape(*dims):
@@ -493,9 +504,9 @@
             f32(8, columns), f32(8, columns), f32(8, columns // 4), f32(8, columns // 4),
             f32(8, columns // 4), f32(8, columns // 4),
             f32(128, 128), f32(rows + 2 * TAPS, KS * 128),
-            f32(tall, group * depth), bf16(tall, group * depth), bf16(tall, group * depth),
-            f32(wide, 8 * rows), bf16(wide, 8 * rows), bf16(wide, 8 * rows),
-            f32(wide, 256), bf16(wide, 256), bf16(wide, 256),
+            f32(tall, group * depth), bf16(tall, 3 * group * depth),
+            f32(wide, 8 * rows), bf16(wide, 24 * rows),
+            f32(wide, 256), bf16(wide, 768),
             bf16(depth, padded + 128), bf16(depth, padded + 128),
             bf16(rows, padded + 128), bf16(rows, padded + 128),
             bf16(32, padded + 128), bf16(32, padded + 128),
@@ -514,6 +525,16 @@
         pixels, basis_kernels, basis_coeffs[0], row_starts, row_taps[0], col_offsets, col_starts, col_taps[0],
         visit_weights, clip_masks[0], jnp.transpose(decorrelation, (1, 0, 2)),
     )
+    wide_block = pl.BlockSpec((rows, columns // 2), lambda n: (0, n))
+    small_block = pl.BlockSpec((rows, width), lambda n: (0, 0))
+    cleaned, template = pl.pallas_call(
+        hand_over,
+        grid=(2,),
+        out_shape=(shape(rows, columns), shape(rows, width)),
+        in_specs=[wide_block, small_block],
+        out_specs=(wide_block, small_block),
+        name="hand_over",
+    )(cleaned, template)
     return (cleaned[None], template)
 
 

time: 44 us -> 43.2 us (0.982)
  local copies, waits for them, and re-layouts: 2.53 us -> 0 us
  Pallas kernels: 39.3 us -> 41.1 us
    unnamed x4 -> x0, local copies, waits for them, and re-layouts: 2.53 us -> none
    pallas_call x0 -> x1, Pallas kernels: none -> 1.82 us  [on_device(): pl.pallas_call(hand_over, grid=(2,), out_shape=(shape(rows, columns), sha...]
where the time goes in v2:
time: 43.2 us; the launch traced here: 43.1 us
  Pallas kernels  41.1 us (95%)
  between operations  1.93 us (4%)
    pallas_call x1, Pallas kernels, on_device(): pl.pallas_call(functools.partial(whole_kernel, nv, nr), out_shape=(shape(...  39.3 us
    pallas_call x1, Pallas kernels, on_device(): pl.pallas_call(hand_over, grid=(2,), out_shape=(shape(rows, columns), sha...  1.82 us

profile of v2, /device:TPU:0, one launch (start us, length us, event | category | flops | bytes accessed | tf_op | source)
XLA Modules:
  0.0 43.1 jit_solution(7821178920453775878)
XLA Ops:
  1.9 39.3 %whole.1 = (f32[32,4096]{1,0:T(8,128)}, f32[32,512]{1,0:T(8,128)}) custom-call(f32[32,4096]{1,0:T(8,128)} %bitcast.7, f32[9,21,21]{2,1,0:T(8,128)} %basis.1, f32[9]{0:T(128)} %bitcast.12, s32[1,32]{1,0:T(1,128)} %row_starts.1, f32[8,32]{1,0:T(8,128)} %bitcast.11, s32[1]{0:T(128)S(6)} %copy.13.offsets, s32[1,4096]{1,0:T(1,128)} %col_starts.1, ...), custom_call_target="tpu_custom_call" | custom-call | tf_op jit(solution)/shard_map/whole/pallas_call | solution.py:494
  41.2 1.8 %hand_over.1 = (f32[32,4096]{1,0:T(8,128)}, f32[32,512]{1,0:T(8,128)}) custom-call(f32[32,4096]{1,0:T(8,128)} %get-tuple-element.6.cleaned, f32[32,512]{1,0:T(8,128)} %get-tuple-element.7.template), custom_call_target="tpu_custom_call" | custom-call | tf_op jit(solution)/shard_map/hand_over/pallas_call | solution.py:530

commit v3 on v2

--- a/solution.py
+++ b/solution.py
@@ -130,7 +130,7 @@
     return copies
 
 
-def scatter_sum(nv, blocks, landed, pair_copies, sums, arrived, sems):
+def scatter_start(nv, blocks, landed, pair_copies, sums, arrived, sems):
     v, r = lax.axis_index("visit"), lax.axis_index("row")
     half = nv // 2
     parity, mine = v % 2, v // 2
@@ -142,6 +142,12 @@
         copy = remote(sums.at[d - 1], arrived.at[d - 1], sems.at[0, d], sems.at[1, d], (2 * k + parity, r))
         copy.start()
         copies.append(copy)
+    return copies
+
+
+def scatter_finish(nv, blocks, landed, pair_copies, arrived, copies):
+    v = lax.axis_index("visit")
+    half, mine = nv // 2, v // 2
     pair_copies[0].wait()
     total = blocks[v] + landed[mine]
     for d in range(1, half):
@@ -256,6 +262,8 @@
         flat[a * rows : (a + 1) * rows, b * depth : (b + 1) * depth] = folded[:, c * 128 : c * 128 + depth]
     store_both(both, flat[...])
 
+    weight_sums = scatter_start(nv, shares, d_landed, weight_pairs, d_sums, d_arrived, d_sum)
+
     kernel_t = kernel_transposed(decor[:, 0, :], square)
     flat_own[...] = jnp.zeros_like(flat_own)
     flat_edge[...] = jnp.zeros_like(flat_edge)
@@ -272,7 +280,6 @@
     for frame in (high, low, second_high, second_low, edge_high, edge_low):
         frame[...] = jnp.zeros_like(frame)
     shifted[...] = jnp.zeros_like(shifted)
-    denominator[...] = scatter_sum(nv, shares, d_landed, weight_pairs, d_sums, d_arrived, d_sum)
 
     tiles = jnp.full((rows, width + 384), dither // 128, jnp.int32)
     place = lax.broadcasted_iota(jnp.int32, (256, 128), 0) - lax.broadcasted_iota(jnp.int32, (256, 128), 1)
@@ -362,6 +369,7 @@
     while done_forwards < half:
         forward(done_forwards)
         done_forwards += 1
+    denominator[...] = scatter_finish(nv, shares, d_landed, weight_pairs, d_arrived, weight_sums)
 
     total = n_sums[mine]
     for d in range(1, half):

time: 43.2 us -> 41.6 us (0.963)
  Pallas kernels: 41.1 us -> 39.5 us
    pallas_call x1, Pallas kernels: 39.3 us -> 37.7 us  [on_device(): pl.pallas_call(functools.partial(whole_kernel, nv, nr), out_shape=(shape(...]
where the time goes in v3:
time: 41.6 us; the launch traced here: 41.4 us
  Pallas kernels  39.5 us (95%)
  between operations  1.93 us (5%)
    pallas_call x1, Pallas kernels, on_device(): pl.pallas_call(functools.partial(whole_kernel, nv, nr), out_shape=(shape(...  37.7 us
    pallas_call x1, Pallas kernels, on_device(): pl.pallas_call(hand_over, grid=(2,), out_shape=(shape(rows, columns), sha...  1.82 us

profile of v3, /device:TPU:0, one launch (start us, length us, event | category | flops | bytes accessed | tf_op | source)
XLA Modules:
  0.0 41.4 jit_solution(3245477847275255679)
XLA Ops:
  1.9 37.7 %whole.1 = (f32[32,4096]{1,0:T(8,128)}, f32[32,512]{1,0:T(8,128)}) custom-call(f32[32,4096]{1,0:T(8,128)} %bitcast.7, f32[9,21,21]{2,1,0:T(8,128)} %basis.1, f32[9]{0:T(128)} %bitcast.12, s32[1,32]{1,0:T(1,128)} %row_starts.1, f32[8,32]{1,0:T(8,128)} %bitcast.11, s32[1]{0:T(128)S(6)} %copy.13.offsets, s32[1,4096]{1,0:T(1,128)} %col_starts.1, ...), custom_call_target="tpu_custom_call" | custom-call | tf_op jit(solution)/shard_map/whole/pallas_call | solution.py:502
  39.6 1.8 %hand_over.1 = (f32[32,4096]{1,0:T(8,128)}, f32[32,512]{1,0:T(8,128)}) custom-call(f32[32,4096]{1,0:T(8,128)} %get-tuple-element.6.cleaned, f32[32,512]{1,0:T(8,128)} %get-tuple-element.7.template), custom_call_target="tpu_custom_call" | custom-call | tf_op jit(solution)/shard_map/hand_over/pallas_call | solution.py:538
